TPU v7x, 512 devices: a whole 4x4x16 slice. The times are simulated.
512 devices in a mesh: section: 16 (over x, z_hi, core), tensor: 32 (over z_lo, y).
Axes of the slice: x: 4, y: 4, z: 16 (z_hi: 2, z_lo: 8; z = z_hi * 8 + z_lo), core: 2. Of those that a mesh axis runs over, the one named last changes fastest.
Arguments:
- context: bfloat16 [16, 256, 4096], P('section', None, 'tensor'), may hold values from -6 to 6
- out_weight: bfloat16 [16, 4096, 8192], P('section', 'tensor'), may hold values from -0.09375 to 0.09375
- residual: bfloat16 [16, 256, 8192], P('section', None, 'tensor'), may hold values from -36 to 36
- gain: float32 [16, 8192], P('section', 'tensor'), may hold values from 0.1 to 1.9
- q_weight: bfloat16 [16, 8192, 4096], P('section', None, 'tensor'), may hold values from -0.044194174 to 0.044194174
- kv_weight: bfloat16 [16, 8192, 1024], P('section', None, 'tensor'), may hold values from -0.044194174 to 0.044194174
Outputs:
- attended: bfloat16 [16, 256, 4096], P('section', None, 'tensor')
All inputs are finite; a program needn't handle non-finite values.
Results may differ from a plain program's by a relative error of at most 0.033.
Values may be sent and summed in bfloat16 or wider, within the bound.
No kernel may reach another device: no remote copies, remote signals or barrier semaphores. Data moves between devices by JAX's collectives and lax.ppermute only.
A program may use at most 64 MiB of HBM per device.

v0:
```python
import jax
import jax.numpy as jnp
from jax import lax
from jax.sharding import PartitionSpec as P

GROUP = 8
THETA = 500000.0


def passed_along(block, axis, distance):
    devices = range(lax.axis_size(axis))
    route = [((i - distance) % len(devices), i) for i in devices]
    return lax.ppermute(block, axis, route)


def rotate(inputs, positions):
    half_width = inputs.shape[-1] // 2
    frequency = THETA ** (-(jnp.arange(half_width).astype(jnp.float32) * 2.0 / inputs.shape[-1]))
    angles = positions[:, None] * frequency[None, :]
    cosine = jnp.cos(angles)[:, None, :]
    sine_part = jnp.sin(angles)[:, None, :]
    first_half = inputs[..., :half_width]
    second_half = inputs[..., half_width:]
    return jnp.concatenate(
        [
            first_half * cosine - second_half * sine_part,
            second_half * cosine + first_half * sine_part,
        ],
        axis=-1,
    )


def on_device(context, out_weight, residual, gain, q_weight, kv_weight):
    local_context = context[0]
    local_out = out_weight[0]
    terms = jnp.dot(local_context, local_out, preferred_element_type=jnp.float32)
    summed = lax.psum_scatter(
        terms.astype(jnp.bfloat16), "tensor", scatter_dimension=1, tiled=True
    ).astype(jnp.float32)
    combined = (residual[0].astype(jnp.float32) + summed).astype(jnp.bfloat16)
    section_gain = gain[0]
    query_cols = q_weight[0]
    pair_cols = kv_weight[0]
    head_size = query_cols.shape[1]
    length = combined.shape[0]
    gathered = lax.all_gather(combined, "tensor", axis=1, tiled=True)
    shifted = passed_along(gathered, "section", 1)
    full_gain = lax.all_gather(section_gain, "tensor", axis=0, tiled=True)
    values_f = shifted.astype(jnp.float32)
    normed = (
        values_f
        * lax.rsqrt(jnp.mean(values_f * values_f, axis=-1, keepdims=True) + 1e-05)
        * full_gain[None, :]
    ).astype(jnp.bfloat16)
    query_proj = jnp.dot(normed, query_cols, preferred_element_type=jnp.float32)
    pair_proj = jnp.dot(normed, pair_cols, preferred_element_type=jnp.float32)
    positions = jnp.arange(length).astype(jnp.float32)
    queries = rotate(query_proj[:, None, :], positions)[:, 0].astype(jnp.bfloat16)
    pair_part = pair_proj.astype(jnp.bfloat16)
    all_pairs = lax.all_gather(pair_part, "tensor", axis=1, tiled=True)
    group_count = lax.axis_size("tensor")
    feature_share = head_size // group_count
    kv_total = pair_cols.shape[1] * group_count // (2 * head_size)
    group_index = lax.axis_index("tensor") // GROUP
    split_cols = all_pairs.reshape(length, group_count, kv_total, 2 * feature_share)
    picked = lax.dynamic_index_in_dim(split_cols, group_index, 2, keepdims=False)
    picked = jnp.transpose(
        picked.reshape(length, group_count, 2, feature_share), (0, 2, 1, 3)
    ).reshape(length, 2, head_size)
    key_rows = rotate(picked[:, 0:1].astype(jnp.float32), positions)[:, 0].astype(jnp.bfloat16)
    values = picked[:, 1]
    scores = jnp.einsum(
        "sd,td->st", queries, key_rows, preferred_element_type=jnp.float32
    ) * head_size ** (-0.5)
    order = jnp.arange(length)
    causal = order[:, None] >= order[None, :]
    scores = jnp.where(causal, scores, -1e30)
    softmax_weights = jax.nn.softmax(scores, axis=-1).astype(jnp.bfloat16)
    attended = jnp.dot(softmax_weights, values, preferred_element_type=jnp.float32).astype(
        jnp.bfloat16
    )
    return attended[None]


def solution(mesh):
    placed = (
        P("section", None, "tensor"),
        P("section", "tensor", None),
        P("section", None, "tensor"),
        P("section", "tensor"),
        P("section", None, "tensor"),
        P("section", None, "tensor"),
    )
    return jax.shard_map(
        on_device,
        mesh=mesh,
        in_specs=placed,
        out_specs=P("section", None, "tensor"),
        check_vma=False,
    )
```

profile of v0, /device:TPU:1, one launch (start us, length us, event | category | flops | bytes accessed | tf_op | source)
XLA Modules:
  0.0 821.7 jit_solution(9606047402175932910)
XLA Ops:
  6.5 0.0 copy-start
  6.5 0.0 copy-start.1
  6.5 0.0 copy-start.2
  6.5 0.0 reduce-scatter.2.cloned.1.call-start
  6.5 1.6 copy-done
  8.1 4.0 convolution_convert_fusion
  12.1 0.0 copy-start.3
  12.1 0.0 reduce-scatter.2.cloned.1.call-update
  12.2 0.0 all-gather.3.cloned.1.call-start
  12.2 227.8 %reduce-scatter.2.cloned.1.call-done = bf16[256,256]{1,0:T(8,128)(2,1)} async-done(((bf16[256,8192]{1,0:T(8,128)(2,1)}), bf16[256,256]{1,0:T(8,128)(2,1)}) %reduce-scatter.2.cloned.1.call-update) | async-done | bytes 131088 | tf_op jit(solution)/shard_map/reduce_scatter | solution.py:37
  240.1 0.0 copy-done.1
  240.1 1.6 fusion.20
  241.7 0.0 all-gather.3.cloned.1.call-update
  241.7 193.1 %all-gather.3.cloned.1.call-done = bf16[256,8192]{1,0:T(8,128)(2,1)} async-done(((bf16[256,256]{1,0:T(8,128)(2,1)}), bf16[256,8192]{1,0:T(8,128)(2,1)}) %all-gather.3.cloned.1.call-update) | async-done | bytes 4194320 | tf_op jit(solution)/shard_map/all_gather | solution.py:46
  434.8 21.0 %collective-permute-start = (bf16[256,8192]{1,0:T(8,128)(2,1)}, bf16[256,8192]{1,0:T(8,128)(2,1)}, u32[]{:S(2)}, u32[]{:S(2)}) collective-permute-start(bf16[256,8192]{1,0:T(8,128)(2,1)} %all-gather.3.cloned.1.call-done), channel_id=1, source_target_pairs={{480,0},{0,32},{32,64},{64,96},{96,128},{128,160},{160,192},{192,2... | collective-permute-start | bytes 12582920 | tf_op jit(solution)/shard_map/ppermute | solution.py:13
  455.8 0.0 copy-done.2
  455.8 245.5 %all-gather = f32[1,8192]{1,0:T(1,128)S(1)} all-gather(f32[1,256]{1,0:T(1,128)S(1)} %copy-done.2), channel_id=2, replica_groups=mesh['section'=16,'tensor'=32] {'tensor'}, dimensions={1}, use_global_device_ids=true | all-gather | bytes 33792 | tf_op jit(solution)/shard_map/all_gather | solution.py:48
  701.3 0.0 collective-permute-done
  701.4 3.1 fusion
  704.5 0.0 copy-done.3
  704.5 3.6 fusion.16
  708.1 100.4 %all_gather.11 = bf16[256,1024]{0,1:T(8,128)(2,1)S(1)} all-gather(bf16[256,32]{0,1:T(8,128)(2,1)S(1)} %fusion.16), channel_id=1, replica_groups=mesh['section'=16,'tensor'=32] {'tensor'}, dimensions={1}, use_global_device_ids=true | all-gather | bytes 540672 | tf_op jit(solution)/shard_map/all_gather | solution.py:60
  808.5 0.1 copy.8
  808.7 4.6 fusion.10
  813.3 0.3 fusion.46
  813.7 0.3 fusion.50
  813.9 0.1 fusion.21
  814.0 0.9 fusion.15
  (7 shorter events, 0.1 us)
Async XLA Ops:
  6.5 1.6 copy-start
  6.5 233.5 %copy-start.1 = (bf16[1,256,256]{2,1,0:T(8,128)(2,1)S(1)}, bf16[1,256,256]{2,1,0:T(8,128)(2,1)}, u32[]{:S(2)}) copy-start(bf16[1,256,256]{2,1,0:T(8,128)(2,1)} %param.8) | copy-start | bytes 393220
  6.5 449.3 %copy-start.2 = (f32[1,256]{1,0:T(1,128)S(1)}, f32[1,256]{1,0:T(1,128)}, u32[]{:S(2)}) copy-start(f32[1,256]{1,0:T(1,128)} %param.9) | copy-start | bytes 3076
  6.5 233.5 %reduce-scatter.2.cloned.1.call-start = ((), (), s32[]{:S(2)}) async-start(), calls=%async_computation.1 | async-start | bytes 4325376 | tf_op jit(solution)/shard_map/reduce_scatter | solution.py:37
  12.1 692.3 %copy-start.3 = (bf16[1,8192,32]{1,2,0:T(8,128)(2,1)S(1)}, bf16[1,8192,32]{1,2,0:T(8,128)(2,1)}, u32[]{:S(2)}) copy-start(bf16[1,8192,32]{1,2,0:T(8,128)(2,1)} %param.11) | copy-start | bytes 1572868
  12.2 422.6 %all-gather.3.cloned.1.call-start = ((), (), s32[]{:S(2)}) async-start(), calls=%async_computation.2 | async-start | bytes 4325376 | tf_op jit(solution)/shard_map/all_gather | solution.py:46
  434.8 266.5 %collective-permute-start = (bf16[256,8192]{1,0:T(8,128)(2,1)}, bf16[256,8192]{1,0:T(8,128)(2,1)}, u32[]{:S(2)}, u32[]{:S(2)}) collective-permute-start(bf16[256,8192]{1,0:T(8,128)(2,1)} %all-gather.3.cloned.1.call-done), channel_id=1, source_target_pairs={{480,0},{0,32},{32,64},{64,96},{96,128},{128,160},{160,192},{192,2... | collective-permute-start | bytes 12582920 | tf_op jit(solution)/shard_map/ppermute | solution.py:13
Sparse Core Ops, SparseCore 0:
  12.3 227.7 reduce-scatter.1
  242.1 192.6 all-gather.2
where the time goes:
time: 822 us
  waiting for transfers between devices  421 us (51%)
  blocking collectives  346 us (42%)
  starting transfers between devices  21 us (3%)
  between operations  13.5 us (2%)
  matrix products  13.4 us (2%)
    all_gather x1, blocking collectives, on_device(): full_gain = lax.all_gather(section_gain, 'tensor', axis=0, tiled=True)  246 us
    reduce_scatter x1, waiting for transfers between devices, on_device(): lax.psum_scatter(terms.astype(jnp.bfloat16), 'tensor', scatter_dimension=...  228 us
    all_gather x1, waiting for transfers between devices, on_device(): gathered = lax.all_gather(combined, 'tensor', axis=1, tiled=True)  193 us
    all_gather x1, blocking collectives, on_device(): all_pairs = lax.all_gather(pair_part, 'tensor', axis=1, tiled=True)  100 us
    ppermute x1, starting transfers between devices, passed_along(): return lax.ppermute(block, axis, route)  21 us
  transfers between devices with their start and end apart: 3, of which 2 were waited for; matrix products, arithmetic and copies ran while one was open for 0% of the time, Pallas kernels for 0%

commit v1 on v0

--- a/solution.py
+++ b/solution.py
@@ -45,7 +45,9 @@
     length = combined.shape[0]
     gathered = lax.all_gather(combined, "tensor", axis=1, tiled=True)
     shifted = passed_along(gathered, "section", 1)
-    full_gain = lax.all_gather(section_gain, "tensor", axis=0, tiled=True)
+    full_gain = jnp.concatenate(
+        lax.all_to_all(jnp.stack([section_gain] * lax.axis_size("tensor")), "tensor", 0, 0), axis=0
+    )
     values_f = shifted.astype(jnp.float32)
     normed = (
         values_f

time: 822 us -> 765 us (0.931); the launches traced: 822 us -> 752 us
  blocking collectives: 346 us -> 107 us
  waiting for transfers between devices: 421 us -> 581 us
  starting transfers between devices: 21 us -> 30.1 us
    all_gather x1 -> x0, blocking collectives: 246 us -> none  [on_device(): full_gain = lax.all_gather(section_gain, 'tensor', axis=0, tiled=True)]
    ppermute x1, waiting for transfers between devices: 0.01 us -> 117 us  [passed_along(): return lax.ppermute(block, axis, route)]
    all_to_all x0 -> x1, waiting for transfers between devices: none -> 42.6 us  [on_device(): lax.all_to_all(jnp.stack([section_gain] * lax.axis_size('tensor')), 'tens...]
    all_to_all x0 -> x1, starting transfers between devices: none -> 9.11 us  [on_device(): lax.all_to_all(jnp.stack([section_gain] * lax.axis_size('tensor')), 'tens...]
  transfers between devices with their start and end apart: 3 -> 4, of which waited for: 2 -> 4; matrix products, arithmetic and copies ran while one was open for 0% -> 0% of each run, Pallas kernels for 0% -> 0%
where the time goes in v1:
time: 765 us; the launch traced here: 752 us
  waiting for transfers between devices  581 us (76%)
  blocking collectives  107 us (14%)
  starting transfers between devices  30.1 us (4%)
  between operations  13.5 us (2%)
  matrix products  13.4 us (2%)
    reduce_scatter x1, waiting for transfers between devices, on_device(): lax.psum_scatter(terms.astype(jnp.bfloat16), 'tensor', scatter_dimension=...  228 us
    all_gather x1, waiting for transfers between devices, on_device(): gathered = lax.all_gather(combined, 'tensor', axis=1, tiled=True)  193 us
    ppermute x1, waiting for transfers between devices, passed_along(): return lax.ppermute(block, axis, route)  117 us
    all_gather x1, blocking collectives, on_device(): all_pairs = lax.all_gather(pair_part, 'tensor', axis=1, tiled=True)  107 us
    all_to_all x1, waiting for transfers between devices, on_device(): lax.all_to_all(jnp.stack([section_gain] * lax.axis_size('tensor')), 'tens...  42.6 us
    ppermute x1, starting transfers between devices, passed_along(): return lax.ppermute(block, axis, route)  21 us
  transfers between devices with their start and end apart: 4, of which 4 were waited for; matrix products, arithmetic and copies ran while one was open for 0% of the time, Pallas kernels for 0%

profile of v1, /device:TPU:1, one launch (start us, length us, event | category | flops | bytes accessed | tf_op | source)
XLA Modules:
  0.0 752.2 jit_solution(1047605716893111867)
XLA Ops:
  6.5 0.0 copy-start
  6.5 0.0 copy-start.1
  6.5 0.0 copy-start.2
  6.5 0.0 reduce-scatter.2.cloned.1.call-start
  6.5 1.6 copy-done
  8.1 4.0 convolution_convert_fusion
  12.2 0.0 copy-start.3
  12.2 0.0 reduce-scatter.2.cloned.1.call-update
  12.2 0.0 all-gather.2.cloned.1.call-start
  12.2 227.8 %reduce-scatter.2.cloned.1.call-done = bf16[256,256]{1,0:T(8,128)(2,1)} async-done(((bf16[256,8192]{1,0:T(8,128)(2,1)}), bf16[256,256]{1,0:T(8,128)(2,1)}) %reduce-scatter.2.cloned.1.call-update) | async-done | bytes 131088 | tf_op jit(solution)/shard_map/reduce_scatter | solution.py:37
  240.1 0.0 copy-done.1
  240.1 1.6 fusion.20
  241.7 0.0 all-gather.2.cloned.1.call-update
  241.7 193.1 %all-gather.2.cloned.1.call-done = bf16[256,8192]{1,0:T(8,128)(2,1)} async-done(((bf16[256,256]{1,0:T(8,128)(2,1)}), bf16[256,8192]{1,0:T(8,128)(2,1)}) %all-gather.2.cloned.1.call-update) | async-done | bytes 4194320 | tf_op jit(solution)/shard_map/all_gather | solution.py:46
  434.8 21.0 %collective-permute-start = (bf16[256,8192]{1,0:T(8,128)(2,1)}, bf16[256,8192]{1,0:T(8,128)(2,1)}, u32[]{:S(2)}, u32[]{:S(2)}) collective-permute-start(bf16[256,8192]{1,0:T(8,128)(2,1)} %all-gather.2.cloned.1.call-done), channel_id=1, source_target_pairs={{480,0},{0,32},{32,64},{64,96},{96,128},{128,160},{160,192},{192,2... | collective-permute-start | bytes 12582920 | tf_op jit(solution)/shard_map/ppermute | solution.py:13
  455.8 0.0 copy-done.2
  455.8 0.6 stack.3
  456.4 9.1 %all-to-all-start = ((f32[32,1,256]{2,1,0:T(1,128)}), f32[32,1,256]{2,1,0:T(1,128)S(1)}, u32[]{:S(2)}, u32[]{:S(2)}) async-start(f32[32,1,256]{2,1,0:T(1,128)} %stack.3), calls=%async_computation.1 | async-start | bytes 65536 | tf_op jit(solution)/shard_map/all_to_all | solution.py:49
  465.6 117.3 %collective-permute-done = bf16[256,8192]{1,0:T(8,128)(2,1)} collective-permute-done((bf16[256,8192]{1,0:T(8,128)(2,1)}, bf16[256,8192]{1,0:T(8,128)(2,1)}, u32[]{:S(2)}, u32[]{:S(2)}) %collective-permute-start) | collective-permute-done | bytes 4194336 | tf_op jit(solution)/shard_map/ppermute | solution.py:13
  582.9 3.1 fusion
  586.0 42.6 %all-to-all-done = f32[32,1,256]{2,1,0:T(1,128)S(1)} async-done(((f32[32,1,256]{2,1,0:T(1,128)}), f32[32,1,256]{2,1,0:T(1,128)S(1)}, u32[]{:S(2)}, u32[]{:S(2)}) %all-to-all-start) | async-done | bytes 32800 | tf_op jit(solution)/shard_map/all_to_all | solution.py:49
  628.7 0.0 copy-done.3
  628.7 3.6 fusion.16
  632.2 106.7 %all_gather.7 = bf16[256,1024]{0,1:T(8,128)(2,1)S(1)} all-gather(bf16[256,32]{0,1:T(8,128)(2,1)S(1)} %fusion.16), channel_id=1, replica_groups=mesh['section'=16,'tensor'=32] {'tensor'}, dimensions={1}, use_global_device_ids=true | all-gather | bytes 540672 | tf_op jit(solution)/shard_map/all_gather | solution.py:62
  739.0 0.1 copy.8
  739.2 4.6 fusion.10
  743.8 0.3 fusion.46
  744.2 0.3 fusion.50
  744.4 0.1 fusion.21
  744.5 0.9 fusion.15
  (7 shorter events, 0.1 us)
Async XLA Ops:
  6.5 1.6 copy-start
  6.5 233.5 %copy-start.1 = (bf16[1,256,256]{2,1,0:T(8,128)(2,1)S(1)}, bf16[1,256,256]{2,1,0:T(8,128)(2,1)}, u32[]{:S(2)}) copy-start(bf16[1,256,256]{2,1,0:T(8,128)(2,1)} %param.8) | copy-start | bytes 393220
  6.5 449.2 %copy-start.2 = (f32[1,256]{1,0:T(1,128)S(1)}, f32[1,256]{1,0:T(1,128)}, u32[]{:S(2)}) copy-start(f32[1,256]{1,0:T(1,128)} %param.9) | copy-start | bytes 3076
  6.5 233.5 %reduce-scatter.2.cloned.1.call-start = ((), (), s32[]{:S(2)}) async-start(), calls=%async_computation.2 | async-start | bytes 4325376 | tf_op jit(solution)/shard_map/reduce_scatter | solution.py:37
  12.2 616.5 %copy-start.3 = (bf16[1,8192,32]{1,2,0:T(8,128)(2,1)S(1)}, bf16[1,8192,32]{1,2,0:T(8,128)(2,1)}, u32[]{:S(2)}) copy-start(bf16[1,8192,32]{1,2,0:T(8,128)(2,1)} %param.11) | copy-start | bytes 1572868
  12.2 422.6 %all-gather.2.cloned.1.call-start = ((), (), s32[]{:S(2)}) async-start(), calls=%async_computation.3 | async-start | bytes 4325376 | tf_op jit(solution)/shard_map/all_gather | solution.py:46
  434.8 148.1 %collective-permute-start = (bf16[256,8192]{1,0:T(8,128)(2,1)}, bf16[256,8192]{1,0:T(8,128)(2,1)}, u32[]{:S(2)}, u32[]{:S(2)}) collective-permute-start(bf16[256,8192]{1,0:T(8,128)(2,1)} %all-gather.2.cloned.1.call-done), channel_id=1, source_target_pairs={{480,0},{0,32},{32,64},{64,96},{96,128},{128,160},{160,192},{192,2... | collective-permute-start | bytes 12582920 | tf_op jit(solution)/shard_map/ppermute | solution.py:13
  456.4 172.2 %all-to-all-start = ((f32[32,1,256]{2,1,0:T(1,128)}), f32[32,1,256]{2,1,0:T(1,128)S(1)}, u32[]{:S(2)}, u32[]{:S(2)}) async-start(f32[32,1,256]{2,1,0:T(1,128)} %stack.3), calls=%async_computation.1 | async-start | bytes 65536 | tf_op jit(solution)/shard_map/all_to_all | solution.py:49
Sparse Core Ops, SparseCore 0:
  12.3 227.7 reduce-scatter.1
  242.1 192.6 all-gather.1
